TPU v7x, 32 devices: a whole 2x2x4 slice. The times are simulated.
32 devices in a mesh: section: 2 (over x), dp: 4 (over z), mp: 4 (over y, core).
Axes of the slice: x: 2, y: 2, z: 4, core: 2. Of those that a mesh axis runs over, the one named last changes fastest.
Arguments:
- hidden: bfloat16 [2, 512, 4096], P('section', 'dp'), may hold values from -9 to 9
- norm_gain: float32 [2, 4096], P('section'), may hold values from 0.5 to 1.5
- kv_weight: bfloat16 [2, 4096, 2048], P('section', None, 'mp'), may hold values from -1 to 1
- attn_flat: bfloat16 [2, 4, 8388608], P('section', 'mp', 'dp'), may hold values from -1 to 1
- final_gain: float32 [4096], replicated, may hold values from 0.5 to 1.5
- reward_head: float32 [4096], replicated, may hold values from -0.09375 to 0.09375
- segment_ids: int32 [2, 4], P('section'), may hold values from 0 to 2, never falling along the last dimension, each value on 1 to 2 neighbouring positions
- ranks: int32 [2], replicated, may hold values from 0 to 999
Outputs:
- next_hidden: bfloat16 [2, 512, 4096], P('section', 'dp')
- rewards: float32 [2], replicated
- pair_loss: float32 [2, 2], replicated
Inputs may be any that keep to these rules, and one draw needn't show every extreme that they name: `segment_ids`: each row's segment numbers never fall, every number of 0 to 2 is present, each on 1 to 2 blocks, one on exactly 2.
All inputs are finite; a program needn't handle non-finite values.
Results may differ from a plain program's by a relative error of at most 0.035.
Values may be sent and summed in bfloat16 or wider, within the bound.
A program may use at most 128 MiB of HBM per device.

v0:
```python
import jax
import jax.numpy as jnp
from jax import lax
from jax.sharding import PartitionSpec as P

HD = 128
QH = 32
KVH = 8
EPS = 1e-05


def passed_along(block, axis, distance):
    devices = range(lax.axis_size(axis))
    route = [(i - distance, i) for i in devices if i - distance in devices]
    return lax.ppermute(block, axis, route)


def shards(hidden, norm_gain, kv_weight, attn_flat, final_gain, reward_head, segment_ids, ranks):
    state = hidden[0]
    tokens = state.shape[0]
    width = state.shape[1]
    seg_row = segment_ids[0]
    blocks = lax.axis_size("dp")
    block = lax.axis_index("dp")
    phases = lax.axis_size("section")
    phase_now = lax.axis_index("section")
    responses = ranks.shape[0]
    state_wide = state.astype(jnp.float32)
    normed = (
        state_wide
        * lax.rsqrt(jnp.mean(state_wide * state_wide, -1, keepdims=True) + EPS)
        * norm_gain[0]
    ).astype(jnp.bfloat16)
    keyval = jnp.dot(normed, kv_weight[0], preferred_element_type=jnp.float32).astype(jnp.bfloat16)
    kv_local = keyval.shape[1] // (2 * HD)
    group = QH // KVH
    q_width = kv_local * group * HD
    flat = lax.all_gather(attn_flat[0, 0], "dp", axis=0, tiled=True)
    w_query = flat[: width * q_width].reshape(width, q_width)
    w_out = flat[width * q_width : 2 * width * q_width].reshape(q_width, width)
    query = jnp.dot(normed, w_query, preferred_element_type=jnp.float32).astype(jnp.bfloat16)
    query = query.reshape(tokens, kv_local, group, HD)
    block_ids = jnp.arange(blocks, dtype=jnp.int32)
    own_seg = jnp.sum(jnp.where(block_ids == block, seg_row, 0))
    query_pos = block * tokens + jnp.arange(tokens, dtype=jnp.int32)
    piece = lax.all_gather(keyval, "dp", axis=0, tiled=True)
    peak = jnp.full((kv_local, group, tokens), -1e30, jnp.float32)
    count = piece.shape[0]
    key_pos = jnp.arange(count, dtype=jnp.int32)
    key_block = key_pos // tokens
    key_seg = jnp.sum(jnp.where(key_block[:, None] == block_ids[None, :], seg_row[None, :], 0), 1)
    parts = piece.reshape(count, kv_local, 2, HD)
    keys = parts[:, :, 0]
    values = parts[:, :, 1]
    earlier = (key_block < block) & (key_block >= 0) & ((key_seg == 0) | (key_seg == own_seg))
    same = (key_block == block)[None, :] & (key_pos[None, :] <= query_pos[:, None])
    visible = earlier[None, :] | same
    scores = jnp.einsum("tjgd,cjd->jgtc", query, keys, preferred_element_type=jnp.float32) * HD ** (
        -0.5
    )
    scores = jnp.where(visible[None, None], scores, -1e30)
    new_peak = jnp.maximum(peak, jnp.max(scores, -1))
    weights = jnp.where(visible[None, None], jnp.exp(scores - new_peak[..., None]), 0.0)
    total = jnp.sum(weights, -1)
    accum = jnp.einsum(
        "jgtc,cjd->jgtd", weights.astype(jnp.bfloat16), values, preferred_element_type=jnp.float32
    )
    peak, total, accum = (new_peak, total, accum)
    mixed = (
        (accum / total[..., None])
        .transpose(2, 0, 1, 3)
        .reshape(tokens, q_width)
        .astype(jnp.bfloat16)
    )
    partial_value = jnp.dot(mixed, w_out, preferred_element_type=jnp.float32)
    ends = (
        jnp.sum(
            (seg_row[None, :] <= jnp.arange(1, responses + 1, dtype=jnp.int32)[:, None]).astype(
                jnp.int32
            ),
            1,
        )
        - 1
    )
    at_end = (ends == block) & (phase_now == phases - 1)
    summed = lax.psum(partial_value.astype(jnp.bfloat16), "mp").astype(jnp.float32)
    updated = (state_wide + summed).astype(jnp.bfloat16)
    moved = passed_along(updated, "section", 1)
    last_row = updated[tokens - 1].astype(jnp.float32)
    squares = jnp.sum(last_row * last_row)
    product = jnp.sum(last_row * final_gain * reward_head)
    sums_sq, dots = lax.psum(
        (jnp.where(at_end, squares, 0.0), jnp.where(at_end, product, 0.0)), ("section", "dp")
    )
    rewards = dots * lax.rsqrt(sums_sq / width + EPS)
    pair_loss = jnp.where(
        ranks[:, None] < ranks[None, :], jax.nn.softplus(rewards[None, :] - rewards[:, None]), 0.0
    )
    return (moved[None], rewards, pair_loss)


def solution(mesh):
    placed = (
        P("section", "dp", None),
        P("section", None),
        P("section", None, "mp"),
        P("section", "mp", "dp"),
        P(),
        P(),
        P("section", None),
        P(),
    )
    return jax.shard_map(
        shards,
        mesh=mesh,
        in_specs=placed,
        out_specs=(P("section", "dp", None), P(), P()),
        check_vma=False,
    )
```

profile of v0, /device:TPU:0, one launch (start us, length us, event | category | flops | bytes accessed | tf_op | source)
XLA Modules:
  0.0 864.1 jit_solution(7415746184136145379)
XLA Ops:
  7.2 0.7 all-gather.3.cloned.1.call-update
  8.7 2.9 fusion.16
  11.6 17.4 %all_gather.6 = bf16[512,512]{1,0:T(8,128)(2,1)S(1)} all-gather(bf16[128,512]{1,0:T(8,128)(2,1)S(1)} %fusion.16), channel_id=1, replica_groups=mesh['section'=2,'dp'=4,'mp'=4] {'dp'}, dimensions={0}, use_global_device_ids=true | all-gather | bytes 655360 | tf_op jit(solution)/shard_map/all_gather | solution.py:46
  29.1 0.7 fusion.48
  29.9 0.7 copy.22
  30.6 0.6 fusion.44
  31.3 0.7 or_and_fusion
  32.2 541.5 %all-gather.3.cloned.1.call-done = bf16[1,1,8388608]{2,1,0:T(2,128)(2,1)} async-done(((bf16[1,1,2097152]{2,1,0:T(2,128)(2,1)}), bf16[1,1,8388608]{2,1,0:T(2,128)(2,1)}) %all-gather.3.cloned.1.call-update) | async-done | bytes 16777232 | tf_op jit(solution)/shard_map/all_gather | solution.py:38
  573.7 183.8 %slice_reduce_fusion = (bf16[4194304]{0:T(1024)(128)(2,1)}, bf16[4194304]{0:T(1024)(128)(2,1)}) fusion(bf16[1,1,8388608]{2,1,0:T(2,128)(2,1)} %all-gather.3.cloned.1.call-done), kind=kLoop, calls=%fused_computation | loop fusion | bytes 33554432 | tf_op jit(solution)/shard_map/slice | solution.py:40
  757.6 13.3 %slice.40 = bf16[1024,4096]{1,0:T(8,128)(2,1)} reshape(bf16[4194304]{0:T(1024)(128)(2,1)} %get-tuple-element.3) | data formatting | bytes 16777216 | tf_op jit(solution)/shard_map/slice | solution.py:40
  770.9 13.3 %slice.37 = bf16[4096,1024]{1,0:T(8,128)(2,1)} reshape(bf16[4194304]{0:T(1024)(128)(2,1)} %get-tuple-element.4) | data formatting | bytes 16777216 | tf_op jit(solution)/shard_map/slice | solution.py:39
  784.2 4.7 convolution_convert_fusion.1
  789.5 0.5 fusion.12
  790.1 0.7 fusion.15
  790.7 1.7 copy-done
  792.4 2.3 convolution_convert_fusion
  794.9 34.2 %all-reduce.3.cloned.1.call-done = bf16[128,4096]{1,0:T(8,128)(2,1)} async-done(((bf16[128,4096]{1,0:T(8,128)(2,1)}), bf16[128,4096]{1,0:T(8,128)(2,1)}) %all-reduce.3.cloned.1.call-update) | async-done | bytes 1048592 | tf_op jit(solution)/shard_map/psum | solution.py:86
  829.1 1.5 fusion.8
  830.6 3.4 collective-permute-start
  834.1 0.6 multiply_reduce_fusion
  834.7 1.3 broadcast_select_fusion
  836.0 19.5 %all-reduce = (f32[2]{0:T(128)S(1)}, f32[2]{0:T(128)S(1)}) all-reduce(f32[2]{0:T(128)S(1)} %get-tuple-element.12, f32[2]{0:T(128)S(1)} %get-tuple-element.11), channel_id=1, replica_groups=mesh['section'=2,'dp'=4,'mp'=4] {'section','dp'}, use_global_device_ids=true, to_apply=%region_8.9 | all-reduce | flops 4 | bytes 32 | tf_op jit(solution)/shard_map/psum | solution.py:92
  855.5 0.7 compare_select_fusion.1
  856.3 1.0 copy.34
  (33 shorter events, 2.2 us)
Async XLA Ops:
  7.2 1.2 copy-start.1
  7.2 1.5 copy-start.7
  7.2 566.5 %all-gather.3.cloned.1.call-start = ((), (), s32[]{:S(2)}) async-start(), calls=%async_computation.1 | async-start | bytes 41943040 | tf_op jit(solution)/shard_map/all_gather | solution.py:38
  7.9 821.2 %all-reduce.3.cloned.1.call-start = ((), (), s32[]{:S(2)}) async-start(), calls=%async_computation | async-start | bytes 2097152 | tf_op jit(solution)/shard_map/psum | solution.py:86
  29.0 1.6 copy-start.6
  789.0 3.4 copy-start
  794.7 39.4 %copy-start.2 = (f32[4096]{0:T(1024)S(1)}, f32[4096]{0:T(1024)}, u32[]{:S(2)}) copy-start(f32[4096]{0:T(1024)} %param.13) | copy-start | bytes 49156
  794.7 39.4 %copy-start.3 = (f32[4096]{0:T(1024)S(1)}, f32[4096]{0:T(1024)}, u32[]{:S(2)}) copy-start(f32[4096]{0:T(1024)} %param.12) | copy-start | bytes 49156
  794.7 60.9 %copy-start.4 = (s32[2]{0:T(128)S(1)}, s32[2]{0:T(128)}, u32[]{:S(2)}) copy-start(s32[2]{0:T(128)} %param.15) | copy-start | bytes 28
  830.6 25.7 %collective-permute-start = (bf16[128,4096]{1,0:T(8,128)(2,1)S(1)}, bf16[128,4096]{1,0:T(8,128)(2,1)S(1)}, u32[]{:S(2)}, u32[]{:S(2)}) collective-permute-start(bf16[128,4096]{1,0:T(8,128)(2,1)S(1)} %fusion.8), channel_id=1, source_target_pairs={{0,16},{1,17},{2,18},{3,19},{4,20},{5,21},{6,22},{7,23},{8,24},{9,... | collective-permute-start | bytes 3145736 | tf_op jit(solution)/shard_map/ppermute | solution.py:15
  855.5 1.8 copy-start.5
Sparse Core Ops, SparseCore 0:
  9.6 564.0 all-gather.2
  794.8 34.2 all-reduce.2
where the time goes:
time: 865 us; the launch traced here: 864 us
  waiting for transfers between devices  577 us (67%)
  local copies, waits for them, and re-layouts  215 us (25%)
  blocking collectives  36.9 us (4%)
  between operations  14.3 us (2%)
  matrix products  11 us (1%)
    all_gather x1, waiting for transfers between devices, shards(): flat = lax.all_gather(attn_flat[0, 0], 'dp', axis=0, tiled=True)  542 us
    slice x2, local copies, waits for them, and re-layouts, shards(): w_out = flat[width * q_width:2 * width * q_width].reshape(q_width, width)  197 us
    psum x1, waiting for transfers between devices, shards(): lax.psum(partial_value.astype(jnp.bfloat16), 'mp').astype(jnp.float32)  34.2 us
    psum x1, blocking collectives, shards(): lax.psum((jnp.where(at_end, squares, 0.0), jnp.where(at_end, product, 0.0...  19.5 us
    all_gather x1, blocking collectives, shards(): piece = lax.all_gather(keyval, 'dp', axis=0, tiled=True)  17.4 us
  transfers between devices with their start and end apart: 3, of which 3 were waited for; matrix products, arithmetic and copies ran while one was open for 1% of the time, Pallas kernels for 0%

commit v1 on v0

--- a/solution.py
+++ b/solution.py
@@ -90,7 +90,8 @@
     squares = jnp.sum(last_row * last_row)
     product = jnp.sum(last_row * final_gain * reward_head)
     sums_sq, dots = lax.psum(
-        (jnp.where(at_end, squares, 0.0), jnp.where(at_end, product, 0.0)), ("section", "dp")
+        lax.psum((jnp.where(at_end, squares, 0.0), jnp.where(at_end, product, 0.0)), "dp"),
+        "section",
     )
     rewards = dots * lax.rsqrt(sums_sq / width + EPS)
     pair_loss = jnp.where(

time: 865 us -> 866 us (level)
  transfers between devices with their start and end apart: 3 -> 3, of which waited for: 3 -> 2; matrix products, arithmetic and copies ran while one was open for 1% -> 1% of each run, Pallas kernels for 0% -> 0%
where the time goes in v1:
time: 866 us; the launch traced here: 865 us
  waiting for transfers between devices  576 us (67%)
  local copies, waits for them, and re-layouts  215 us (25%)
  blocking collectives  37.4 us (4%)
  between operations  14.2 us (2%)
  matrix products  11 us (1%)
    all_gather x1, waiting for transfers between devices, shards(): flat = lax.all_gather(attn_flat[0, 0], 'dp', axis=0, tiled=True)  542 us
    slice x2, local copies, waits for them, and re-layouts, shards(): w_out = flat[width * q_width:2 * width * q_width].reshape(q_width, width)  197 us
    psum x1, waiting for transfers between devices, shards(): lax.psum(partial_value.astype(jnp.bfloat16), 'mp').astype(jnp.float32)  34.2 us
    all_gather x1, blocking collectives, shards(): piece = lax.all_gather(keyval, 'dp', axis=0, tiled=True)  17.4 us
  transfers between devices with their start and end apart: 3, of which 2 were waited for; matrix products, arithmetic and copies ran while one was open for 1% of the time, Pallas kernels for 0%

profile of v1, /device:TPU:0, one launch (start us, length us, event | category | flops | bytes accessed | tf_op | source)
XLA Modules:
  0.0 864.5 jit_solution(10173166650345601188)
XLA Ops:
  7.2 0.7 all-gather.3.cloned.1.call-update
  8.7 2.9 fusion.16
  11.6 17.4 %all_gather.6 = bf16[512,512]{1,0:T(8,128)(2,1)S(1)} all-gather(bf16[128,512]{1,0:T(8,128)(2,1)S(1)} %fusion.16), channel_id=1, replica_groups=mesh['section'=2,'dp'=4,'mp'=4] {'dp'}, dimensions={0}, use_global_device_ids=true | all-gather | bytes 655360 | tf_op jit(solution)/shard_map/all_gather | solution.py:46
  29.1 0.7 fusion.48
  29.9 0.7 copy.22
  30.6 0.6 fusion.44
  31.3 0.7 or_and_fusion
  32.2 541.5 %all-gather.3.cloned.1.call-done = bf16[1,1,8388608]{2,1,0:T(2,128)(2,1)} async-done(((bf16[1,1,2097152]{2,1,0:T(2,128)(2,1)}), bf16[1,1,8388608]{2,1,0:T(2,128)(2,1)}) %all-gather.3.cloned.1.call-update) | async-done | bytes 16777232 | tf_op jit(solution)/shard_map/all_gather | solution.py:38
  573.7 183.8 %slice_reduce_fusion = (bf16[4194304]{0:T(1024)(128)(2,1)}, bf16[4194304]{0:T(1024)(128)(2,1)}) fusion(bf16[1,1,8388608]{2,1,0:T(2,128)(2,1)} %all-gather.3.cloned.1.call-done), kind=kLoop, calls=%fused_computation | loop fusion | bytes 33554432 | tf_op jit(solution)/shard_map/slice | solution.py:40
  757.6 13.3 %slice.40 = bf16[1024,4096]{1,0:T(8,128)(2,1)} reshape(bf16[4194304]{0:T(1024)(128)(2,1)} %get-tuple-element.3) | data formatting | bytes 16777216 | tf_op jit(solution)/shard_map/slice | solution.py:40
  770.9 13.3 %slice.37 = bf16[4096,1024]{1,0:T(8,128)(2,1)} reshape(bf16[4194304]{0:T(1024)(128)(2,1)} %get-tuple-element.4) | data formatting | bytes 16777216 | tf_op jit(solution)/shard_map/slice | solution.py:39
  784.2 4.7 convolution_convert_fusion.1
  790.1 0.7 fusion.15
  790.7 1.7 copy-done
  792.4 2.3 convolution_convert_fusion
  794.9 34.2 %all-reduce.4.cloned.1.call-done = bf16[128,4096]{1,0:T(8,128)(2,1)} async-done(((bf16[128,4096]{1,0:T(8,128)(2,1)}), bf16[128,4096]{1,0:T(8,128)(2,1)}) %all-reduce.4.cloned.1.call-update) | async-done | bytes 1048592 | tf_op jit(solution)/shard_map/psum | solution.py:86
  829.1 1.5 fusion.8
  830.6 3.4 collective-permute-start
  834.1 0.6 multiply_reduce_fusion
  834.7 1.3 broadcast_select_fusion
  836.0 11.7 %all-reduce = (f32[2]{0:T(128)S(1)}, f32[2]{0:T(128)S(1)}) all-reduce(f32[2]{0:T(128)S(1)} %get-tuple-element.14, f32[2]{0:T(128)S(1)} %get-tuple-element.13), channel_id=1, replica_groups=mesh['section'=2,'dp'=4,'mp'=4] {'dp'}, use_global_device_ids=true, to_apply=%region_8.9 | all-reduce | flops 4 | bytes 32 | tf_op jit(solution)/shard_map/psum | solution.py:93
  847.7 8.3 all-reduce.1
  856.1 0.7 compare_select_fusion.1
  856.7 1.0 copy.34
  (34 shorter events, 2.6 us)
Async XLA Ops:
  7.2 1.2 copy-start.1
  7.2 1.5 copy-start.7
  7.2 566.5 %all-gather.3.cloned.1.call-start = ((), (), s32[]{:S(2)}) async-start(), calls=%async_computation.1 | async-start | bytes 41943040 | tf_op jit(solution)/shard_map/all_gather | solution.py:38
  7.9 821.2 %all-reduce.4.cloned.1.call-start = ((), (), s32[]{:S(2)}) async-start(), calls=%async_computation | async-start | bytes 2097152 | tf_op jit(solution)/shard_map/psum | solution.py:86
  29.0 1.6 copy-start.6
  789.0 3.4 copy-start
  794.7 39.4 %copy-start.2 = (f32[4096]{0:T(1024)S(1)}, f32[4096]{0:T(1024)}, u32[]{:S(2)}) copy-start(f32[4096]{0:T(1024)} %param.13) | copy-start | bytes 49156
  794.7 39.4 %copy-start.3 = (f32[4096]{0:T(1024)S(1)}, f32[4096]{0:T(1024)}, u32[]{:S(2)}) copy-start(f32[4096]{0:T(1024)} %param.12) | copy-start | bytes 49156
  794.7 61.4 %copy-start.4 = (s32[2]{0:T(128)S(1)}, s32[2]{0:T(128)}, u32[]{:S(2)}) copy-start(s32[2]{0:T(128)} %param.15) | copy-start | bytes 28
  830.6 26.1 %collective-permute-start = (bf16[128,4096]{1,0:T(8,128)(2,1)S(1)}, bf16[128,4096]{1,0:T(8,128)(2,1)S(1)}, u32[]{:S(2)}, u32[]{:S(2)}) collective-permute-start(bf16[128,4096]{1,0:T(8,128)(2,1)S(1)} %fusion.8), channel_id=1, source_target_pairs={{0,16},{1,17},{2,18},{3,19},{4,20},{5,21},{6,22},{7,23},{8,24},{9,... | collective-permute-start | bytes 3145736 | tf_op jit(solution)/shard_map/ppermute | solution.py:15
  856.1 1.6 copy-start.5
Sparse Core Ops, SparseCore 0:
  9.6 564.0 all-gather.2
  794.8 34.2 all-reduce.3
